TPU v7x, 256 devices: a whole 4x4x8 slice. The times are simulated.
256 devices in a mesh: group: 4 (over y), shard: 64 (over x, z, core).
Axes of the slice: x: 4, y: 4, z: 8, core: 2. Of those that a mesh axis runs over, the one named last changes fastest.
Arguments:
- activations: bfloat16 [4, 128, 256, 1024], P('group', 'shard'), may hold values from -7 to 7
- out_grad: bfloat16 [4, 128, 256, 1024], P('group', None, 'shard'), may hold values from -1.5 to 1.5
- embedding: bfloat16 [512, 1024], replicated, may hold values from -6 to 6
- counts: int32 [4, 8], P('group'), may hold values from 0 to 256, as said below
- offsets: int32 [4, 8], P('group'), may hold values from 0 to 8, as said below
- layout: int32 [4, 256], P('group'), may hold values from 0 to 511
Outputs:
- input_grad: bfloat16 [4, 128, 256, 1024], P('group', 'shard')
- embedding_grad: float32 [512, 1024], P('group')
Inputs may be any that keep to these rules, and one draw needn't show every extreme that they name: `counts`: A used session slot holds 19 to 256 electrodes; slots after the used ones hold 0. `offsets`: used session slots come first; the first starts at block 0 and each next one where the previous ends, a session taking ceil(count / 32) blocks, all sessions together exactly 8 blocks; unused slots hold 8.
All inputs are finite; a program needn't handle non-finite values.
Results may differ from a plain program's by a relative error of at most 0.012.
The roundings to bfloat16 on the way count: a program that leaves them out, or rounds other values in their place, can miss the bound.
Values may be sent and summed in bfloat16 or wider, within the bound.
A program may use at most 64 MiB of HBM per device.

v0:
```python
import math
import jax
import jax.numpy as jnp
from jax import lax
from jax.sharding import PartitionSpec as P

HEADS = 16
BLOCK = 32


def product(form, left, right):
    return jnp.einsum(form, left, right, preferred_element_type=jnp.float32)


def attend(values, allowed):
    length = values.shape[0]
    head_split = values.reshape(length, HEADS, -1)
    score_scale = 0.5 / math.sqrt(head_split.shape[-1])
    scores = product("qhd,khd->hqk", head_split, head_split) * score_scale
    scores = jnp.where(allowed[None], scores, -1e30)
    row_max = jnp.max(scores, axis=-1, keepdims=True)
    exponent = jnp.exp(scores - row_max)
    weights = (exponent / jnp.sum(exponent, axis=-1, keepdims=True)).astype(jnp.bfloat16)
    attended = product("hqk,khd->qhd", weights, head_split)
    return (head_split, weights, attended)


def attend_back(values, allowed, cotangent):
    head_split, weights, attended = attend(values, allowed)
    length = values.shape[0]
    score_scale = 0.5 / math.sqrt(head_split.shape[-1])
    grad_heads = cotangent.reshape(length, HEADS, -1)
    row_delta = jnp.sum(grad_heads.astype(jnp.float32) * attended, axis=-1)
    grad_weights = product("qhd,khd->hqk", grad_heads, head_split)
    grad_scores = (
        weights.astype(jnp.float32) * (grad_weights - jnp.transpose(row_delta)[:, :, None])
    ).astype(jnp.bfloat16)
    grad_values = score_scale * (
        product("hqk,khd->qhd", grad_scores, head_split)
        + product("hqk,qhd->khd", grad_scores, head_split)
    )
    grad_values = grad_values + product("hqk,qhd->khd", weights, grad_heads)
    return grad_values.reshape(length, -1)


def session_pairs(counts, offsets, electrodes):
    slot_index = jnp.arange(electrodes, dtype=jnp.int32)
    block_index = slot_index // BLOCK
    member = (offsets[None, :] <= block_index[:, None]).astype(jnp.int32)
    session = jnp.sum(member, axis=1) - 1
    chosen = (jnp.arange(offsets.shape[0], dtype=jnp.int32)[None, :] == session[:, None]).astype(
        jnp.int32
    )
    first_slot = jnp.sum(chosen * offsets[None, :], axis=1) * BLOCK
    live_count = jnp.sum(chosen * counts[None, :], axis=1)
    is_live = slot_index - first_slot < live_count
    return (session[:, None] == session[None, :]) & is_live[None, :]


def body(activations, out_grad, embedding, counts, offsets, layout):
    local_in = activations[0]
    electrodes = local_in.shape[1]
    templates = embedding.shape[0]
    allowed = session_pairs(counts[0], offsets[0], electrodes)
    onehot = (layout[0][:, None] == jnp.arange(templates, dtype=jnp.int32)[None, :]).astype(
        jnp.bfloat16
    )
    layout_rows = jnp.dot(onehot, embedding, preferred_element_type=jnp.float32)
    embedded = (local_in.astype(jnp.float32) + layout_rows[None]).astype(jnp.bfloat16)

    def spatial(values):
        return (
            values.astype(jnp.float32) + attend(values, allowed)[2].reshape(electrodes, -1)
        ).astype(jnp.bfloat16)

    mixed = lax.map(spatial, embedded)
    gathered = lax.all_to_all(mixed[None], "shard", split_axis=2, concat_axis=1, tiled=True)
    patches = gathered.shape[1]
    full_mask = jnp.ones((patches, patches), dtype=bool)

    def temporal(couple):
        values, cotangent = couple
        return (cotangent.astype(jnp.float32) + attend_back(values, full_mask, cotangent)).astype(
            jnp.bfloat16
        )

    mixed_grad = lax.map(
        temporal, (jnp.moveaxis(gathered[0], 1, 0), jnp.moveaxis(out_grad[0], 1, 0))
    )
    returned = lax.all_to_all(
        jnp.moveaxis(mixed_grad, 0, 1)[None], "shard", split_axis=1, concat_axis=2, tiled=True
    )

    def spatial_back(couple):
        values, cotangent = couple
        return cotangent.astype(jnp.float32) + attend_back(values, allowed, cotangent)

    full_grad = lax.map(spatial_back, (embedded, returned[0]))
    input_grad = full_grad.astype(jnp.bfloat16)[None]
    electrode_grad = jnp.sum(full_grad, axis=0)
    shards = lax.axis_size("shard")
    groups = lax.axis_size("group")
    width = local_in.shape[2]
    pieces = jnp.transpose(electrode_grad).astype(jnp.bfloat16)
    pieces = pieces.reshape(shards, width // shards, electrodes)
    arrived = lax.all_to_all(pieces, "shard", split_axis=0, concat_axis=0, tiled=True)
    own_columns = jnp.sum(arrived.astype(jnp.float32), axis=0)
    column_table = jnp.dot(
        own_columns.astype(jnp.bfloat16), onehot, preferred_element_type=jnp.float32
    )
    own_rows = templates // groups
    column_table = column_table.reshape(width // shards, groups, own_rows)
    from_groups = lax.all_to_all(
        jnp.moveaxis(column_table, 1, 0), "group", split_axis=0, concat_axis=0, tiled=True
    )
    own_part = jnp.sum(from_groups, axis=0)
    gathered_table = lax.all_gather(own_part, "shard", axis=0, tiled=True)
    table_grad = jnp.transpose(gathered_table)
    return (input_grad, table_grad)


def solution(mesh):
    placed = (
        P("group", "shard", None, None),
        P("group", None, "shard", None),
        P(),
        P("group", None),
        P("group", None),
        P("group", None),
    )
    return jax.shard_map(
        body,
        mesh=mesh,
        in_specs=placed,
        out_specs=(P("group", "shard", None, None), P("group", None)),
        check_vma=False,
    )
```

profile of v0, /device:TPU:1, one launch (start us, length us, event | category | flops | bytes accessed | tf_op | source)
XLA Modules:
  0.0 249.8 jit_solution(14660771344484138781)
XLA Ops:
  5.3 14.4 %while.33 = (s32[]{:T(128)}, bf16[2,256,1024]{1,2,0:T(8,128)(2,1)}, bf16[2,256,1024]{1,2,0:T(8,128)(2,1)S(1)}, s32[256]{0:T(256)S(1)}, pred[256]{0:T(512)(128)(4,1)S(1)}, /*index=5*/s32[]{:T(128)}) while((s32[]{:T(128)}, bf16[2,256,1024]{1,2,0:T(8,128)(2,1)}, bf16[2,256,1024]{1,2,0:T(8,128)(2,1)S(1)}, s32[256]{0:T(256)S(1)}, ...), condition=%wide.region_6.7_spmd.clone, body=%wide.region_3.6_spmd.clone.sunk | while | flops 275644672 | bytes 13797193 | solution.py:76
  5.5 3.4 %fusion.140 = (f32[16,256]{1,0:T(8,128)S(1)}, f32[16,256,256]{1,2,0:T(8,128)}) fusion(pred[256,256]{0,1:T(8,128)(4,1)S(1)} %compare_and_fusion.4, bf16[256,16,64]{0,2,1:T(8,128)(2,1)S(1)} %bitcast.190), kind=kOutput, calls=%fused_computation.86.clone.1 | convolution fusion | flops 138412288 | bytes 4800512 | tf_op jit(solution)/shard_map/while/body/eval_jaxpr/sub | solution.py:22
  8.9 2.7 %fusion.141 = f32[16,64,256]{2,1,0:T(8,128)S(1)} fusion(bf16[256,16,64]{0,2,1:T(8,128)(2,1)S(1)} %bitcast.191, f32[16,256,256]{1,2,0:T(8,128)} %get-tuple-element.283, f32[16,256]{1,0:T(8,128)S(1)} %get-tuple-element.284), kind=kOutput, calls=%fused_computation.30.clone.1 | convolution fusion | flops 136314880 | bytes 5783552 | tf_op jit(solution)/shard_map/while/body/eval_jaxpr/hqk,khd->qhd/dot_general | solution.py:12
  12.7 3.4 %fusion.140 = (f32[16,256]{1,0:T(8,128)S(1)}, f32[16,256,256]{1,2,0:T(8,128)}) fusion(pred[256,256]{0,1:T(8,128)(4,1)S(1)} %compare_and_fusion.4, bf16[256,16,64]{0,2,1:T(8,128)(2,1)S(1)} %bitcast.190), kind=kOutput, calls=%fused_computation.86.clone.1 | convolution fusion | flops 138412288 | bytes 4800512 | tf_op jit(solution)/shard_map/while/body/eval_jaxpr/sub | solution.py:22
  16.1 2.7 %fusion.141 = f32[16,64,256]{2,1,0:T(8,128)S(1)} fusion(bf16[256,16,64]{0,2,1:T(8,128)(2,1)S(1)} %bitcast.191, f32[16,256,256]{1,2,0:T(8,128)} %get-tuple-element.283, f32[16,256]{1,0:T(8,128)S(1)} %get-tuple-element.284), kind=kOutput, calls=%fused_computation.30.clone.1 | convolution fusion | flops 136314880 | bytes 5783552 | tf_op jit(solution)/shard_map/while/body/eval_jaxpr/hqk,khd->qhd/dot_general | solution.py:12
  19.7 3.7 %copy.82 = bf16[2,256,1024]{2,0,1:T(2,128)(2,1)} copy(bf16[2,256,1024]{1,2,0:T(8,128)(2,1)} %get-tuple-element.73) | data formatting | bytes 2097152 | tf_op jit(solution)/shard_map/while | solution.py:76
  23.5 13.0 %all-to-all-start = ((bf16[1,2,256,1024]{3,1,0,2:T(2,128)(2,1)}), bf16[1,2,256,1024]{3,1,0,2:T(2,128)(2,1)S(1)}, u32[]{:S(2)}, u32[]{:S(2)}) async-start(bf16[1,2,256,1024]{3,1,0,2:T(2,128)(2,1)} %bitcast.195), calls=%async_computation | async-start | bytes 2097152 | tf_op jit(solution)/shard_map/all_to_all | solution.py:77
  36.5 2.7 %copy.79 = bf16[1,128,4,1024]{1,3,2,0:T(8,128)(2,1)} copy(bf16[1,128,4,1024]{3,2,1,0:T(4,128)(2,1)} %param.13) | data formatting | bytes 2097152 | tf_op args[1]
  39.1 25.8 %all-to-all-done = bf16[1,2,256,1024]{3,1,0,2:T(2,128)(2,1)S(1)} async-done(((bf16[1,2,256,1024]{3,1,0,2:T(2,128)(2,1)}), bf16[1,2,256,1024]{3,1,0,2:T(2,128)(2,1)S(1)}, u32[]{:S(2)}, u32[]{:S(2)}) %all-to-all-start) | async-done | bytes 1048608 | tf_op jit(solution)/shard_map/all_to_all | solution.py:77
  65.0 1.5 copy.83
  66.5 2.7 %copy.84 = bf16[4,128,1024]{1,2,0:T(8,128)(2,1)} copy(bf16[4,128,1024]{2,0,1:T(4,128)(2,1)} %bitcast.197) | data formatting | bytes 2097152 | tf_op jit(solution)/shard_map/while | solution.py:87
  69.2 26.1 %while.32 = (s32[]{:T(128)}, bf16[4,128,1024]{1,2,0:T(8,128)(2,1)}, bf16[4,128,1024]{1,2,0:T(8,128)(2,1)}, bf16[4,128,1024]{1,2,0:T(8,128)(2,1)}, s32[]{:T(128)}) while((s32[]{:T(128)}, bf16[4,128,1024]{1,2,0:T(8,128)(2,1)}, bf16[4,128,1024]{1,2,0:T(8,128)(2,1)}, bf16[4,128,1024]{1,2,0:T(8,128)(2,1)}, s32[]{:T(128)}) %tuple.88), condition=%wide.region_11.12_spmd, body=%wide.region_7.11_spmd.sunk | while | flops 204863616 | bytes 12616257 | solution.py:87
  70.3 1.5 fusion.132
  76.8 1.5 fusion.132
  83.3 1.5 fusion.132
  95.3 2.7 %copy.85 = bf16[4,128,1024]{2,0,1:T(4,128)(2,1)} copy(bf16[4,128,1024]{1,2,0:T(8,128)(2,1)} %get-tuple-element.74) | data formatting | bytes 2097152 | tf_op jit(solution)/shard_map/while | solution.py:87
  98.0 6.2 %all-to-all-start.1 = ((bf16[1,128,4,1024]{3,2,0,1:T(4,128)(2,1)}), bf16[1,128,4,1024]{3,2,0,1:T(4,128)(2,1)S(1)}, u32[]{:S(2)}, u32[]{:S(2)}) async-start(bf16[1,128,4,1024]{3,2,0,1:T(4,128)(2,1)} %bitcast.196), calls=%async_computation.1 | async-start | bytes 2097152 | tf_op jit(solution)/shard_map/all_to_all | solution.py:90
  104.2 28.5 %all-to-all-done.1 = bf16[1,128,4,1024]{3,2,0,1:T(4,128)(2,1)S(1)} async-done(((bf16[1,128,4,1024]{3,2,0,1:T(4,128)(2,1)}), bf16[1,128,4,1024]{3,2,0,1:T(4,128)(2,1)S(1)}, u32[]{:S(2)}, u32[]{:S(2)}) %all-to-all-start.1) | async-done | bytes 1048608 | tf_op jit(solution)/shard_map/all_to_all | solution.py:90
  132.7 2.1 copy.86
  134.8 3.6 %copy.87 = bf16[2,256,1024]{1,2,0:T(8,128)(2,1)} copy(bf16[2,256,1024]{2,0,1:T(2,128)(2,1)} %bitcast.198) | data formatting | bytes 2097152
  138.4 23.5 %while.34 = (s32[]{:T(128)}, f32[2,256,1024]{1,2,0:T(8,128)}, bf16[2,256,1024]{1,2,0:T(8,128)(2,1)}, bf16[2,256,1024]{1,2,0:T(8,128)(2,1)S(1)}, s32[256]{0:T(256)S(1)}, /*index=5*/pred[256]{0:T(512)(128)(4,1)S(1)}, s32[]{:T(128)}) while((s32[]{:T(128)}, f32[2,256,1024]{1,2,0:T(8,128)}, bf16[2,256,1024]{1,2,0:T(8,128)(2,1)}, ...), condition=%wide.region_16.17_spmd.clone, body=%wide.region_12.16_spmd.clone.sunk | while | flops 818016512 | bytes 37422928 | solution.py:98
  139.6 3.4 %fusion.154 = (f32[16,256]{1,0:T(8,128)S(1)}, f32[16,256,256]{1,2,0:T(8,128)}) fusion(pred[256,256]{0,1:T(8,128)(4,1)S(1)} %compare_and_fusion.5, bf16[256,16,64]{0,2,1:T(8,128)(2,1)S(1)} %bitcast.174), kind=kOutput, calls=%fused_computation.87.clone.1 | convolution fusion | flops 138412288 | bytes 4800512 | tf_op jit(solution)/shard_map/while/body/eval_jaxpr/sub | solution.py:22
  143.1 2.6 %divide_convert_fusion.9 = bf16[16,256,256]{1,2,0:T(8,128)(2,1)S(1)} fusion(f32[16,256,256]{1,2,0:T(8,128)} %get-tuple-element.292, f32[16,256]{1,0:T(8,128)S(1)} %get-tuple-element.293), kind=kLoop, calls=%fused_computation.42.clone.1 | loop fusion | flops 2097152 | bytes 6307840 | tf_op jit(solution)/shard_map/while/body/eval_jaxpr/convert_element_type | solution.py:23
  151.4 3.4 %fusion.154 = (f32[16,256]{1,0:T(8,128)S(1)}, f32[16,256,256]{1,2,0:T(8,128)}) fusion(pred[256,256]{0,1:T(8,128)(4,1)S(1)} %compare_and_fusion.5, bf16[256,16,64]{0,2,1:T(8,128)(2,1)S(1)} %bitcast.174), kind=kOutput, calls=%fused_computation.87.clone.1 | convolution fusion | flops 138412288 | bytes 4800512 | tf_op jit(solution)/shard_map/while/body/eval_jaxpr/sub | solution.py:22
  154.8 2.6 %divide_convert_fusion.9 = bf16[16,256,256]{1,2,0:T(8,128)(2,1)S(1)} fusion(f32[16,256,256]{1,2,0:T(8,128)} %get-tuple-element.292, f32[16,256]{1,0:T(8,128)S(1)} %get-tuple-element.293), kind=kLoop, calls=%fused_computation.42.clone.1 | loop fusion | flops 2097152 | bytes 6307840 | tf_op jit(solution)/shard_map/while/body/eval_jaxpr/convert_element_type | solution.py:23
  161.9 2.7 %reduce_sum.105 = bf16[256,1024]{0,1:T(8,128)(2,1)} reduce(f32[2,256,1024]{1,2,0:T(8,128)} %get-tuple-element.75, f32[]{:T(128)} %constant.80.clone.1), dimensions={0}, to_apply=%region_17.18 | reduce | flops 262144 | bytes 2621444 | tf_op jit(solution)/shard_map/reduce_sum | solution.py:100
  164.6 6.2 %all-to-all-start.2 = ((bf16[64,16,256]{2,1,0:T(8,128)(2,1)}), bf16[64,16,256]{2,1,0:T(8,128)(2,1)S(1)}, u32[]{:S(2)}, u32[]{:S(2)}) async-start(bf16[64,16,256]{2,1,0:T(8,128)(2,1)} %bitcast.24), calls=%async_computation.2 | async-start | bytes 1048576 | tf_op jit(solution)/shard_map/all_to_all | solution.py:106
  170.8 17.3 %all-to-all-done.2 = bf16[64,16,256]{2,1,0:T(8,128)(2,1)S(1)} async-done(((bf16[64,16,256]{2,1,0:T(8,128)(2,1)}), bf16[64,16,256]{2,1,0:T(8,128)(2,1)S(1)}, u32[]{:S(2)}, u32[]{:S(2)}) %all-to-all-start.2) | async-done | bytes 524320 | tf_op jit(solution)/shard_map/all_to_all | solution.py:106
  189.1 4.2 %all-to-all-start.3 = ((f32[4,16,128]{2,1,0:T(8,128)}), f32[4,16,128]{2,1,0:T(8,128)S(1)}, u32[]{:S(2)}, u32[]{:S(2)}) async-start(f32[4,16,128]{2,1,0:T(8,128)} %convolution_bitcast_fusion.2), calls=%async_computation.3 | async-start | bytes 65536 | tf_op jit(solution)/shard_map/all_to_all | solution.py:113
  193.3 2.5 %copy.88 = bf16[2,256,1024]{2,1,0:T(8,128)(2,1)} copy(f32[2,256,1024]{1,2,0:T(8,128)} %get-tuple-element.75) | data formatting | bytes 3145728 | tf_op jit(solution)/shard_map/while | solution.py:98
  195.8 1.8 all-to-all-done.3
  197.6 51.2 %all_gather.3 = f32[1024,128]{1,0:T(8,128)S(1)} all-gather(f32[16,128]{1,0:T(8,128)S(1)} %reduce_sum.107), channel_id=1, replica_groups=mesh['group'=4,'shard'=64] {'shard'}, dimensions={0}, use_global_device_ids=true | all-gather | bytes 532480 | tf_op jit(solution)/shard_map/all_gather | solution.py:117
  (75 shorter events, 41.8 us)
Async XLA Ops:
  0.6 3.1 %copy-start = (bf16[512,1024]{1,0:T(8,128)(2,1)S(1)}, bf16[512,1024]{1,0:T(8,128)(2,1)}, u32[]{:S(2)}) copy-start(bf16[512,1024]{1,0:T(8,128)(2,1)} %param.14) | copy-start | bytes 3145732
  23.5 41.5 %all-to-all-start = ((bf16[1,2,256,1024]{3,1,0,2:T(2,128)(2,1)}), bf16[1,2,256,1024]{3,1,0,2:T(2,128)(2,1)S(1)}, u32[]{:S(2)}, u32[]{:S(2)}) async-start(bf16[1,2,256,1024]{3,1,0,2:T(2,128)(2,1)} %bitcast.195), calls=%async_computation | async-start | bytes 2097152 | tf_op jit(solution)/shard_map/all_to_all | solution.py:77
  98.0 34.7 %all-to-all-start.1 = ((bf16[1,128,4,1024]{3,2,0,1:T(4,128)(2,1)}), bf16[1,128,4,1024]{3,2,0,1:T(4,128)(2,1)S(1)}, u32[]{:S(2)}, u32[]{:S(2)}) async-start(bf16[1,128,4,1024]{3,2,0,1:T(4,128)(2,1)} %bitcast.196), calls=%async_computation.1 | async-start | bytes 2097152 | tf_op jit(solution)/shard_map/all_to_all | solution.py:90
  161.9 26.3 %copy-start.1 = (s32[1,256]{1,0:T(1,128)S(1)}, s32[1,256]{1,0:T(1,128)}, u32[]{:S(2)}) copy-start(s32[1,256]{1,0:T(1,128)} %param.17) | copy-start | bytes 3076
  164.6 23.5 %all-to-all-start.2 = ((bf16[64,16,256]{2,1,0:T(8,128)(2,1)}), bf16[64,16,256]{2,1,0:T(8,128)(2,1)S(1)}, u32[]{:S(2)}, u32[]{:S(2)}) async-start(bf16[64,16,256]{2,1,0:T(8,128)(2,1)} %bitcast.24), calls=%async_computation.2 | async-start | bytes 1048576 | tf_op jit(solution)/shard_map/all_to_all | solution.py:106
  189.1 8.5 %all-to-all-start.3 = ((f32[4,16,128]{2,1,0:T(8,128)}), f32[4,16,128]{2,1,0:T(8,128)S(1)}, u32[]{:S(2)}, u32[]{:S(2)}) async-start(f32[4,16,128]{2,1,0:T(8,128)} %convolution_bitcast_fusion.2), calls=%async_computation.3 | async-start | bytes 65536 | tf_op jit(solution)/shard_map/all_to_all | solution.py:113
where the time goes:
time: 251 us; the launch traced here: 250 us
  waiting for transfers between devices  73.4 us (29%)
  blocking collectives  51.2 us (20%)
  matrix products  41.2 us (16%)
  local copies, waits for them, and re-layouts  30.6 us (12%)
  starting transfers between devices  29.5 us (12%)
  other arithmetic  22.9 us (9%)
    all_gather x1, blocking collectives, body(): gathered_table = lax.all_gather(own_part, 'shard', axis=0, tiled=True)  51.2 us
    all_to_all x1, waiting for transfers between devices, body(): lax.all_to_all(jnp.moveaxis(mixed_grad, 0, 1)[None], 'shard', split_axis=...  28.5 us
    all_to_all x1, waiting for transfers between devices, body(): lax.all_to_all(mixed[None], 'shard', split_axis=2, concat_axis=1, tiled=T...  25.8 us
    sub x8, matrix products, attend(): exponent = jnp.exp(scores - row_max)  19.6 us
    dot_general x32, matrix products, product(): return jnp.einsum(form, left, right, preferred_element_type=jnp.float32)  19.4 us
    all_to_all x1, waiting for transfers between devices, body(): lax.all_to_all(pieces, 'shard', split_axis=0, concat_axis=0, tiled=True)  17.3 us
    all_to_all x1, starting transfers between devices, body(): lax.all_to_all(mixed[None], 'shard', split_axis=2, concat_axis=1, tiled=T...  13 us
    convert_element_type x6, other arithmetic, attend(): (exponent / jnp.sum(exponent, axis=-1, keepdims=True)).astype(jnp.bfloat16)  10.6 us
  transfers between devices with their start and end apart: 4, of which 4 were waited for; matrix products, arithmetic and copies ran while one was open for 2% of the time, Pallas kernels for 0%

commit v1 on v0

--- a/solution.py
+++ b/solution.py
@@ -114,7 +114,9 @@
         jnp.moveaxis(column_table, 1, 0), "group", split_axis=0, concat_axis=0, tiled=True
     )
     own_part = jnp.sum(from_groups, axis=0)
-    gathered_table = lax.all_gather(own_part, "shard", axis=0, tiled=True)
+    gathered_table = jnp.concatenate(
+        lax.all_to_all(jnp.stack([own_part] * lax.axis_size("shard")), "shard", 0, 0), axis=0
+    )
     table_grad = jnp.transpose(gathered_table)
     return (input_grad, table_grad)
 

time: 251 us -> 225 us (0.90)
  blocking collectives: 51.2 us -> 8.29 us
  waiting for transfers between devices: 73.4 us -> 86.4 us
  starting transfers between devices: 29.5 us -> 33.1 us
    all_gather x1 -> x0, blocking collectives: 51.2 us -> none  [body(): gathered_table = lax.all_gather(own_part, 'shard', axis=0, tiled=True)]
    all_to_all x1, waiting for transfers between devices: 1.76 us -> 14.7 us  [body(): lax.all_to_all(jnp.stack([own_part] * lax.axis_size('shard')), 'shard', 0...]
    all_to_all x0 -> x1, blocking collectives: none -> 8.29 us  [body(): lax.all_to_all(jnp.moveaxis(column_table, 1, 0), 'group', split_axis=0, c...]
    all_to_all x1, starting transfers between devices: 4.19 us -> 7.72 us  [body(): lax.all_to_all(jnp.stack([own_part] * lax.axis_size('shard')), 'shard', 0...]
where the time goes in v1:
time: 225 us; the launch traced here: 224 us
  waiting for transfers between devices  86.4 us (38%)
  matrix products  40.5 us (18%)
  starting transfers between devices  33.1 us (15%)
  local copies, waits for them, and re-layouts  31.4 us (14%)
  other arithmetic  22.9 us (10%)
  blocking collectives  8.29 us (4%)
    all_to_all x1, waiting for transfers between devices, body(): lax.all_to_all(jnp.moveaxis(mixed_grad, 0, 1)[None], 'shard', split_axis=...  28.5 us
    all_to_all x1, waiting for transfers between devices, body(): lax.all_to_all(mixed[None], 'shard', split_axis=2, concat_axis=1, tiled=T...  25.8 us
    sub x8, matrix products, attend(): exponent = jnp.exp(scores - row_max)  19.6 us
    dot_general x32, matrix products, product(): return jnp.einsum(form, left, right, preferred_element_type=jnp.float32)  19.4 us
    all_to_all x1, waiting for transfers between devices, body(): lax.all_to_all(pieces, 'shard', split_axis=0, concat_axis=0, tiled=True)  17.3 us
    all_to_all x1, waiting for transfers between devices, body(): lax.all_to_all(jnp.stack([own_part] * lax.axis_size('shard')), 'shard', 0...  14.7 us
    all_to_all x1, starting transfers between devices, body(): lax.all_to_all(mixed[None], 'shard', split_axis=2, concat_axis=1, tiled=T...  13 us
    convert_element_type x6, other arithmetic, attend(): (exponent / jnp.sum(exponent, axis=-1, keepdims=True)).astype(jnp.bfloat16)  10.6 us
  transfers between devices with their start and end apart: 4, of which 4 were waited for; matrix products, arithmetic and copies ran while one was open for 2% of the time, Pallas kernels for 0%

profile of v1, /device:TPU:1, one launch (start us, length us, event | category | flops | bytes accessed | tf_op | source)
XLA Modules:
  0.0 223.6 jit_solution(470595126102113410)
XLA Ops:
  5.3 14.4 %while.33 = (s32[]{:T(128)}, bf16[2,256,1024]{1,2,0:T(8,128)(2,1)}, bf16[2,256,1024]{1,2,0:T(8,128)(2,1)S(1)}, s32[256]{0:T(256)S(1)}, pred[256]{0:T(512)(128)(4,1)S(1)}, /*index=5*/s32[]{:T(128)}) while((s32[]{:T(128)}, bf16[2,256,1024]{1,2,0:T(8,128)(2,1)}, bf16[2,256,1024]{1,2,0:T(8,128)(2,1)S(1)}, s32[256]{0:T(256)S(1)}, ...), condition=%wide.region_6.7_spmd.clone, body=%wide.region_3.6_spmd.clone.sunk | while | flops 275644672 | bytes 13797193 | solution.py:76
  5.5 3.4 %fusion.140 = (f32[16,256]{1,0:T(8,128)S(1)}, f32[16,256,256]{1,2,0:T(8,128)}) fusion(pred[256,256]{0,1:T(8,128)(4,1)S(1)} %compare_and_fusion.4, bf16[256,16,64]{0,2,1:T(8,128)(2,1)S(1)} %bitcast.192), kind=kOutput, calls=%fused_computation.86.clone.1 | convolution fusion | flops 138412288 | bytes 4800512 | tf_op jit(solution)/shard_map/while/body/eval_jaxpr/sub | solution.py:22
  8.9 2.7 %fusion.141 = f32[16,64,256]{2,1,0:T(8,128)S(1)} fusion(bf16[256,16,64]{0,2,1:T(8,128)(2,1)S(1)} %bitcast.193, f32[16,256,256]{1,2,0:T(8,128)} %get-tuple-element.285, f32[16,256]{1,0:T(8,128)S(1)} %get-tuple-element.286), kind=kOutput, calls=%fused_computation.30.clone.1 | convolution fusion | flops 136314880 | bytes 5783552 | tf_op jit(solution)/shard_map/while/body/eval_jaxpr/hqk,khd->qhd/dot_general | solution.py:12
  12.7 3.4 %fusion.140 = (f32[16,256]{1,0:T(8,128)S(1)}, f32[16,256,256]{1,2,0:T(8,128)}) fusion(pred[256,256]{0,1:T(8,128)(4,1)S(1)} %compare_and_fusion.4, bf16[256,16,64]{0,2,1:T(8,128)(2,1)S(1)} %bitcast.192), kind=kOutput, calls=%fused_computation.86.clone.1 | convolution fusion | flops 138412288 | bytes 4800512 | tf_op jit(solution)/shard_map/while/body/eval_jaxpr/sub | solution.py:22
  16.1 2.7 %fusion.141 = f32[16,64,256]{2,1,0:T(8,128)S(1)} fusion(bf16[256,16,64]{0,2,1:T(8,128)(2,1)S(1)} %bitcast.193, f32[16,256,256]{1,2,0:T(8,128)} %get-tuple-element.285, f32[16,256]{1,0:T(8,128)S(1)} %get-tuple-element.286), kind=kOutput, calls=%fused_computation.30.clone.1 | convolution fusion | flops 136314880 | bytes 5783552 | tf_op jit(solution)/shard_map/while/body/eval_jaxpr/hqk,khd->qhd/dot_general | solution.py:12
  19.7 3.7 %copy.83 = bf16[2,256,1024]{2,0,1:T(2,128)(2,1)} copy(bf16[2,256,1024]{1,2,0:T(8,128)(2,1)} %get-tuple-element.73) | data formatting | bytes 2097152 | tf_op jit(solution)/shard_map/while | solution.py:76
  23.5 13.0 %all-to-all-start = ((bf16[1,2,256,1024]{3,1,0,2:T(2,128)(2,1)}), bf16[1,2,256,1024]{3,1,0,2:T(2,128)(2,1)S(1)}, u32[]{:S(2)}, u32[]{:S(2)}) async-start(bf16[1,2,256,1024]{3,1,0,2:T(2,128)(2,1)} %bitcast.197), calls=%async_computation | async-start | bytes 2097152 | tf_op jit(solution)/shard_map/all_to_all | solution.py:77
  36.5 2.7 %copy.80 = bf16[1,128,4,1024]{1,3,2,0:T(8,128)(2,1)} copy(bf16[1,128,4,1024]{3,2,1,0:T(4,128)(2,1)} %param.13) | data formatting | bytes 2097152 | tf_op args[1]
  39.1 25.8 %all-to-all-done = bf16[1,2,256,1024]{3,1,0,2:T(2,128)(2,1)S(1)} async-done(((bf16[1,2,256,1024]{3,1,0,2:T(2,128)(2,1)}), bf16[1,2,256,1024]{3,1,0,2:T(2,128)(2,1)S(1)}, u32[]{:S(2)}, u32[]{:S(2)}) %all-to-all-start) | async-done | bytes 1048608 | tf_op jit(solution)/shard_map/all_to_all | solution.py:77
  65.0 1.5 copy.84
  66.5 2.7 %copy.85 = bf16[4,128,1024]{1,2,0:T(8,128)(2,1)} copy(bf16[4,128,1024]{2,0,1:T(4,128)(2,1)} %bitcast.199) | data formatting | bytes 2097152 | tf_op jit(solution)/shard_map/while | solution.py:87
  69.2 26.1 %while.32 = (s32[]{:T(128)}, bf16[4,128,1024]{1,2,0:T(8,128)(2,1)}, bf16[4,128,1024]{1,2,0:T(8,128)(2,1)}, bf16[4,128,1024]{1,2,0:T(8,128)(2,1)}, s32[]{:T(128)}) while((s32[]{:T(128)}, bf16[4,128,1024]{1,2,0:T(8,128)(2,1)}, bf16[4,128,1024]{1,2,0:T(8,128)(2,1)}, bf16[4,128,1024]{1,2,0:T(8,128)(2,1)}, s32[]{:T(128)}) %tuple.89), condition=%wide.region_11.12_spmd, body=%wide.region_7.11_spmd.sunk | while | flops 204863616 | bytes 12616257 | solution.py:87
  70.3 1.5 fusion.132
  76.8 1.5 fusion.132
  83.3 1.5 fusion.132
  95.3 2.7 %copy.86 = bf16[4,128,1024]{2,0,1:T(4,128)(2,1)} copy(bf16[4,128,1024]{1,2,0:T(8,128)(2,1)} %get-tuple-element.74) | data formatting | bytes 2097152 | tf_op jit(solution)/shard_map/while | solution.py:87
  98.0 6.2 %all-to-all-start.1 = ((bf16[1,128,4,1024]{3,2,0,1:T(4,128)(2,1)}), bf16[1,128,4,1024]{3,2,0,1:T(4,128)(2,1)S(1)}, u32[]{:S(2)}, u32[]{:S(2)}) async-start(bf16[1,128,4,1024]{3,2,0,1:T(4,128)(2,1)} %bitcast.198), calls=%async_computation.1 | async-start | bytes 2097152 | tf_op jit(solution)/shard_map/all_to_all | solution.py:90
  104.2 28.5 %all-to-all-done.1 = bf16[1,128,4,1024]{3,2,0,1:T(4,128)(2,1)S(1)} async-done(((bf16[1,128,4,1024]{3,2,0,1:T(4,128)(2,1)}), bf16[1,128,4,1024]{3,2,0,1:T(4,128)(2,1)S(1)}, u32[]{:S(2)}, u32[]{:S(2)}) %all-to-all-start.1) | async-done | bytes 1048608 | tf_op jit(solution)/shard_map/all_to_all | solution.py:90
  132.7 2.1 copy.87
  134.8 3.6 %copy.88 = bf16[2,256,1024]{1,2,0:T(8,128)(2,1)} copy(bf16[2,256,1024]{2,0,1:T(2,128)(2,1)} %bitcast.200) | data formatting | bytes 2097152
  138.4 23.5 %while.34 = (s32[]{:T(128)}, f32[2,256,1024]{1,2,0:T(8,128)}, bf16[2,256,1024]{1,2,0:T(8,128)(2,1)}, bf16[2,256,1024]{1,2,0:T(8,128)(2,1)S(1)}, s32[256]{0:T(256)S(1)}, /*index=5*/pred[256]{0:T(512)(128)(4,1)S(1)}, s32[]{:T(128)}) while((s32[]{:T(128)}, f32[2,256,1024]{1,2,0:T(8,128)}, bf16[2,256,1024]{1,2,0:T(8,128)(2,1)}, ...), condition=%wide.region_16.17_spmd.clone, body=%wide.region_12.16_spmd.clone.sunk | while | flops 818016512 | bytes 37422928 | solution.py:98
  139.6 3.4 %fusion.154 = (f32[16,256]{1,0:T(8,128)S(1)}, f32[16,256,256]{1,2,0:T(8,128)}) fusion(pred[256,256]{0,1:T(8,128)(4,1)S(1)} %compare_and_fusion.5, bf16[256,16,64]{0,2,1:T(8,128)(2,1)S(1)} %bitcast.176), kind=kOutput, calls=%fused_computation.87.clone.1 | convolution fusion | flops 138412288 | bytes 4800512 | tf_op jit(solution)/shard_map/while/body/eval_jaxpr/sub | solution.py:22
  143.1 2.6 %divide_convert_fusion.9 = bf16[16,256,256]{1,2,0:T(8,128)(2,1)S(1)} fusion(f32[16,256,256]{1,2,0:T(8,128)} %get-tuple-element.294, f32[16,256]{1,0:T(8,128)S(1)} %get-tuple-element.295), kind=kLoop, calls=%fused_computation.42.clone.1 | loop fusion | flops 2097152 | bytes 6307840 | tf_op jit(solution)/shard_map/while/body/eval_jaxpr/convert_element_type | solution.py:23
  151.4 3.4 %fusion.154 = (f32[16,256]{1,0:T(8,128)S(1)}, f32[16,256,256]{1,2,0:T(8,128)}) fusion(pred[256,256]{0,1:T(8,128)(4,1)S(1)} %compare_and_fusion.5, bf16[256,16,64]{0,2,1:T(8,128)(2,1)S(1)} %bitcast.176), kind=kOutput, calls=%fused_computation.87.clone.1 | convolution fusion | flops 138412288 | bytes 4800512 | tf_op jit(solution)/shard_map/while/body/eval_jaxpr/sub | solution.py:22
  154.8 2.6 %divide_convert_fusion.9 = bf16[16,256,256]{1,2,0:T(8,128)(2,1)S(1)} fusion(f32[16,256,256]{1,2,0:T(8,128)} %get-tuple-element.294, f32[16,256]{1,0:T(8,128)S(1)} %get-tuple-element.295), kind=kLoop, calls=%fused_computation.42.clone.1 | loop fusion | flops 2097152 | bytes 6307840 | tf_op jit(solution)/shard_map/while/body/eval_jaxpr/convert_element_type | solution.py:23
  161.9 2.7 %reduce_sum.105 = bf16[256,1024]{0,1:T(8,128)(2,1)} reduce(f32[2,256,1024]{1,2,0:T(8,128)} %get-tuple-element.75, f32[]{:T(128)} %constant.80.clone.1), dimensions={0}, to_apply=%region_17.18 | reduce | flops 262144 | bytes 2621444 | tf_op jit(solution)/shard_map/reduce_sum | solution.py:100
  164.6 6.2 %all-to-all-start.2 = ((bf16[64,16,256]{2,1,0:T(8,128)(2,1)}), bf16[64,16,256]{2,1,0:T(8,128)(2,1)S(1)}, u32[]{:S(2)}, u32[]{:S(2)}) async-start(bf16[64,16,256]{2,1,0:T(8,128)(2,1)} %bitcast.24), calls=%async_computation.2 | async-start | bytes 1048576 | tf_op jit(solution)/shard_map/all_to_all | solution.py:106
  170.8 17.3 %all-to-all-done.2 = bf16[64,16,256]{2,1,0:T(8,128)(2,1)S(1)} async-done(((bf16[64,16,256]{2,1,0:T(8,128)(2,1)}), bf16[64,16,256]{2,1,0:T(8,128)(2,1)S(1)}, u32[]{:S(2)}, u32[]{:S(2)}) %all-to-all-start.2) | async-done | bytes 524320 | tf_op jit(solution)/shard_map/all_to_all | solution.py:106
  188.5 8.3 %all_to_all.45 = f32[4,16,128]{2,1,0:T(8,128)S(1)} all-to-all(f32[4,16,128]{2,1,0:T(8,128)S(1)} %convolution_bitcast_fusion.2), channel_id=1, replica_groups=mesh['group'=4,'shard'=64] {'group'}, dimensions={0} | all-to-all | bytes 65536 | tf_op jit(solution)/shard_map/all_to_all | solution.py:113
  197.6 7.7 %all-to-all-start.4 = ((f32[64,16,128]{2,1,0:T(8,128)}), f32[64,16,128]{2,1,0:T(8,128)S(1)}, u32[]{:S(2)}, u32[]{:S(2)}) async-start(f32[64,16,128]{2,1,0:T(8,128)} %stack.2), calls=%async_computation.4 | async-start | bytes 1048576 | tf_op jit(solution)/shard_map/all_to_all | solution.py:118
  205.3 2.5 %copy.89 = bf16[2,256,1024]{2,1,0:T(8,128)(2,1)} copy(f32[2,256,1024]{1,2,0:T(8,128)} %get-tuple-element.75) | data formatting | bytes 3145728 | tf_op jit(solution)/shard_map/while | solution.py:98
  207.9 14.7 %all-to-all-done.4 = f32[64,16,128]{2,1,0:T(8,128)S(1)} async-done(((f32[64,16,128]{2,1,0:T(8,128)}), f32[64,16,128]{2,1,0:T(8,128)S(1)}, u32[]{:S(2)}, u32[]{:S(2)}) %all-to-all-start.4) | async-done | bytes 524320 | tf_op jit(solution)/shard_map/all_to_all | solution.py:118
  (76 shorter events, 42.0 us)
Async XLA Ops:
  0.6 3.1 %copy-start = (bf16[512,1024]{1,0:T(8,128)(2,1)S(1)}, bf16[512,1024]{1,0:T(8,128)(2,1)}, u32[]{:S(2)}) copy-start(bf16[512,1024]{1,0:T(8,128)(2,1)} %param.14) | copy-start | bytes 3145732
  23.5 41.5 %all-to-all-start = ((bf16[1,2,256,1024]{3,1,0,2:T(2,128)(2,1)}), bf16[1,2,256,1024]{3,1,0,2:T(2,128)(2,1)S(1)}, u32[]{:S(2)}, u32[]{:S(2)}) async-start(bf16[1,2,256,1024]{3,1,0,2:T(2,128)(2,1)} %bitcast.197), calls=%async_computation | async-start | bytes 2097152 | tf_op jit(solution)/shard_map/all_to_all | solution.py:77
  98.0 34.7 %all-to-all-start.1 = ((bf16[1,128,4,1024]{3,2,0,1:T(4,128)(2,1)}), bf16[1,128,4,1024]{3,2,0,1:T(4,128)(2,1)S(1)}, u32[]{:S(2)}, u32[]{:S(2)}) async-start(bf16[1,128,4,1024]{3,2,0,1:T(4,128)(2,1)} %bitcast.198), calls=%async_computation.1 | async-start | bytes 2097152 | tf_op jit(solution)/shard_map/all_to_all | solution.py:90
  161.9 26.3 %copy-start.1 = (s32[1,256]{1,0:T(1,128)S(1)}, s32[1,256]{1,0:T(1,128)}, u32[]{:S(2)}) copy-start(s32[1,256]{1,0:T(1,128)} %param.17) | copy-start | bytes 3076
  164.6 23.5 %all-to-all-start.2 = ((bf16[64,16,256]{2,1,0:T(8,128)(2,1)}), bf16[64,16,256]{2,1,0:T(8,128)(2,1)S(1)}, u32[]{:S(2)}, u32[]{:S(2)}) async-start(bf16[64,16,256]{2,1,0:T(8,128)(2,1)} %bitcast.24), calls=%async_computation.2 | async-start | bytes 1048576 | tf_op jit(solution)/shard_map/all_to_all | solution.py:106
  197.6 25.0 %all-to-all-start.4 = ((f32[64,16,128]{2,1,0:T(8,128)}), f32[64,16,128]{2,1,0:T(8,128)S(1)}, u32[]{:S(2)}, u32[]{:S(2)}) async-start(f32[64,16,128]{2,1,0:T(8,128)} %stack.2), calls=%async_computation.4 | async-start | bytes 1048576 | tf_op jit(solution)/shard_map/all_to_all | solution.py:118
